TPU v7x, 128 devices: a whole 4x4x4 slice. The times are simulated.
128 devices in a mesh: client: 16 (over y_lo, x, core), unit: 8 (over z, y_hi).
Axes of the slice: x: 4, y: 4 (y_hi: 2, y_lo: 2; y = y_hi * 2 + y_lo), z: 4, core: 2. Of those that a mesh axis runs over, the one named last changes fastest.
Arguments:
- token_ids: int32 [256], replicated, may hold values from 0 to 65535
- embed_table: bfloat16 [65536, 4096], P(('client', 'unit')), may hold values from -6 to 6
- norm_gain: float32 [4096], replicated, may hold values from 0.5 to 1.5
- client_gate: bfloat16 [16, 4096, 7168], P('client', None, 'unit'), may hold values from -0.09375 to 0.09375
- client_up: bfloat16 [16, 4096, 7168], P('client', None, 'unit'), may hold values from -0.09375 to 0.09375
- ref_gate: bfloat16 [4096, 7168], P('client', 'unit'), may hold values from -0.09375 to 0.09375
- ref_up: bfloat16 [4096, 7168], P('client', 'unit'), may hold values from -0.09375 to 0.09375
Outputs:
- merged: float32 [7168, 256], P('unit')
- score: float32 [16, 7168], P('client', 'unit')
All inputs are finite; a program needn't handle non-finite values.
Results may differ from a plain program's by a relative error of at most 0.014.
Values may be sent and summed in bfloat16 or wider, within the bound.
A program may use at most 128 MiB of HBM per device.

v0:
```python
import jax
import jax.numpy as jnp
from jax import lax
from jax.sharding import PartitionSpec as P

sharpness = 40.0
block_cols = 2048


def split_up(shard, dim, count):
    before, after = (shard.shape[:dim], shard.shape[dim + 1 :])
    return jnp.moveaxis(shard.reshape(*before, count, -1, *after), dim, 0)


def summed_on_arrival(shard, axis, dim):
    count = lax.axis_size(axis)
    blocks = lax.all_to_all(split_up(shard, dim, count), axis, 0, 0, tiled=True)
    return jnp.sum(blocks, axis=0)


def sent_together(arrays, axis, dim, along):
    widths = [a.shape[along] for a in arrays]
    both = jnp.concatenate(arrays, axis=along)
    result = summed_on_arrival(both, axis, dim)
    return tuple(jnp.split(result, [sum(widths[:k]) for k in range(1, len(widths))], axis=along))


def laid_out(blocks, dim):
    dims = list(blocks.shape[1:])
    dims[dim] *= blocks.shape[0]
    return jnp.moveaxis(blocks, 0, dim).reshape(dims)


def copy_for_each(shard, axis):
    copies = jnp.broadcast_to(shard, (lax.axis_size(axis), *shard.shape))
    return lax.all_to_all(copies, axis, split_axis=0, concat_axis=0, tiled=True)


def gather_directly(shard, axis, dim):
    return laid_out(copy_for_each(shard, axis), dim)


def filled_up(lines, count):
    spare = -len(lines) % count
    return jnp.pad(lines, [(0, spare)] + [(0, 0)] * (lines.ndim - 1))


def sent_and_summed(shard, axis, dim):
    blocks = split_up(shard, dim, lax.axis_size(axis))
    arrived = lax.all_to_all(blocks, axis, split_axis=0, concat_axis=0, tiled=True)
    return arrived.astype(jnp.float32).sum(axis=0)


def nested_sum(shard, axes):
    lines = shard.reshape(-1, shard.shape[-1])
    padded = filled_up(lines, lax.axis_size(axes))
    whole = gather_directly(sent_and_summed(padded, axes, 0).astype(jnp.bfloat16), axes, 0)
    return lax.slice_in_dim(whole, 0, len(lines)).reshape(shard.shape).astype(jnp.float32)


def standardize(hidden):
    center = jnp.mean(hidden, axis=0, keepdims=True)
    shifted = hidden - center
    spread = jnp.sqrt(jnp.mean(shifted * shifted, axis=0, keepdims=True) + 1e-06)
    return (shifted / spread).astype(jnp.bfloat16)


def block_ranges(length):
    return [(offset, min(block_cols, length - offset)) for offset in range(0, length, block_cols)]


def rms_scaled(values, norm_gain):
    scale = lax.rsqrt(jnp.mean(values * values, axis=1, keepdims=True) + 1e-05)
    return (values * scale * norm_gain[None, :]).astype(jnp.bfloat16)


def body(token_ids, embed_table, norm_gain, client_gate, client_up, ref_gate, ref_up):
    rows_here = embed_table.shape[0]
    table_start = (
        lax.axis_index("client") * lax.axis_size("unit") + lax.axis_index("unit")
    ) * rows_here
    table_rows = table_start + jnp.arange(rows_here, dtype=jnp.int32)
    selector = (token_ids[:, None] == table_rows[None, :]).astype(jnp.bfloat16)
    partial_rows = jnp.dot(selector, embed_table, preferred_element_type=jnp.float32)
    embedded = lax.psum(partial_rows, ("client", "unit"))
    normed = rms_scaled(embedded, norm_gain)
    token_count = normed.shape[0]
    inverse_tokens = 1.0 / token_count
    gate_local = jnp.dot(normed, client_gate[0], preferred_element_type=jnp.float32)
    up_local = jnp.dot(normed, client_up[0], preferred_element_type=jnp.float32)
    client_std = standardize(jax.nn.silu(gate_local) * up_local)
    row_span = ref_gate.shape[0]
    normed_slice = lax.dynamic_slice_in_dim(
        normed, lax.axis_index("client") * row_span, row_span, 1
    )
    gate_part = jnp.dot(normed_slice, ref_gate, preferred_element_type=jnp.float32)
    up_part = jnp.dot(normed_slice, ref_up, preferred_element_type=jnp.float32)
    gate_share, up_share = sent_together((gate_part, up_part), "client", 1, 0)
    ref_piece = standardize(jax.nn.silu(gate_share) * up_share)
    ref_std = gather_directly(ref_piece, "client", 1)
    local_units = client_std.shape[1]
    segment = lax.all_gather(client_std, "unit", axis=1, tiled=True)
    numerator = jnp.zeros((local_units, token_count), jnp.float32)
    colsum = jnp.zeros((local_units,), jnp.float32)
    weighted = jnp.zeros((local_units,), jnp.float32)
    for offset, width in block_ranges(segment.shape[1]):
        columns = segment[:, offset : offset + width]
        correlation = (
            jnp.dot(columns.T, ref_std, preferred_element_type=jnp.float32) * inverse_tokens
        )
        weights = jnp.exp(sharpness * correlation)
        numerator = numerator + lax.dot_general(
            weights.astype(jnp.bfloat16),
            columns,
            (((0,), (1,)), ((), ())),
            preferred_element_type=jnp.float32,
        )
        colsum = colsum + jnp.sum(weights, axis=0)
        weighted = weighted + jnp.sum(weights * correlation, axis=0)
    numerator, colsum, weighted = (numerator, colsum, weighted)
    matched = numerator / colsum[:, None]
    score = (weighted / colsum)[None, :]
    merged = nested_sum(matched.astype(jnp.bfloat16), "client") / lax.axis_size("client")
    return (merged, score)


def solution(mesh):
    in_specs = (
        P(),
        P(("client", "unit"), None),
        P(),
        P("client", None, "unit"),
        P("client", None, "unit"),
        P("client", "unit"),
        P("client", "unit"),
    )
    out_specs = (P("unit", None), P("client", "unit"))
    return jax.shard_map(body, mesh=mesh, in_specs=in_specs, out_specs=out_specs, check_vma=False)
```

profile of v0, /device:TPU:1, one launch (start us, length us, event | category | flops | bytes accessed | tf_op | source)
XLA Modules:
  0.0 315.0 jit_solution(14013043354471950132)
XLA Ops:
  7.2 0.0 copy-start
  7.2 0.0 all-reduce.2.cloned.1.call-start
  7.2 5.5 %fusion.51 = f32[256,4096]{1,0:T(8,128)} fusion(bf16[512,4096]{1,0:T(8,128)(2,1)} %param.8, s32[512]{0:T(512)S(1)} %iota_add_fusion, s32[256]{0:T(256)} %param.7), kind=kOutput, calls=%fused_computation.49 | convolution fusion | flops 1073872896 | bytes 8391680 | tf_op jit(solution)/shard_map/dot_general | solution.py:84
  12.8 0.0 all-reduce.2.cloned.1.call-update
  12.8 0.0 all-gather.2.cloned.1.call-start
  12.8 157.7 %all-reduce.2.cloned.1.call-done = f32[256,4096]{1,0:T(8,128)} async-done(((f32[256,4096]{1,0:T(8,128)}), f32[256,4096]{1,0:T(8,128)}) %all-reduce.2.cloned.1.call-update) | async-done | bytes 4194320 | tf_op jit(solution)/shard_map/psum | solution.py:85
  170.5 2.7 multiply_reduce_fusion.3
  173.2 0.0 copy-done.5
  173.2 0.7 copy-done.2
  174.0 0.6 multiply_convert_fusion
  174.5 0.0 slice-start.1
  174.6 5.7 %fusion.2 = f32[256,896]{1,0:T(8,128)S(1)} fusion(bf16[256,4096]{1,0:T(8,128)(2,1)S(1)} %multiply_convert_fusion, bf16[1,4096,896]{2,1,0:T(8,128)(2,1)} %param.10), kind=kOutput, calls=%fused_computation.2 | convolution fusion | flops 1879048192 | bytes 10354688 | tf_op jit(solution)/shard_map/dot_general | solution.py:89
  180.3 0.0 slice-done
  180.3 0.0 slice-done.1
  180.3 2.4 fusion.69
  182.8 0.0 copy-start.4
  182.8 0.1 multiply_reduce_fusion.5
  182.9 0.9 divide_convert_fusion
  183.8 0.0 all-gather.2.cloned.1.call-update
  183.8 0.0 copy-done
  183.8 0.3 fusion.58
  184.1 0.0 copy-done.4
  184.1 0.3 fusion.60
  184.4 0.1 pad_maximum_fusion
  184.6 1.8 copy.9
  186.3 31.7 %all_to_all.20 = f32[16,512,56]{1,2,0:T(8,128)S(1)} all-to-all(f32[16,512,56]{1,2,0:T(8,128)} %bitcast.27), channel_id=1, replica_groups=mesh['client'=16,'unit'=8] {'client'}, dimensions={0} | all-to-all | bytes 3670016 | tf_op jit(solution)/shard_map/all_to_all | solution.py:17
  218.0 0.1 reduce_sum.141
  218.2 0.1 fusion.68
  218.3 0.2 multiply_reduce_fusion.6
  218.5 0.1 divide_convert_fusion.1
  218.6 13.6 %all_to_all.21 = bf16[16,256,56]{1,2,0:T(8,128)(2,1)S(1)} all-to-all(bf16[16,256,56]{1,2,0:T(8,128)(2,1)S(1)} %broadcast_in_dim.4), channel_id=1, replica_groups=mesh['client'=16,'unit'=8] {'client'}, dimensions={0} | all-to-all | bytes 917504 | tf_op jit(solution)/shard_map/all_to_all | solution.py:36
  232.2 32.9 %all-gather.2.cloned.1.call-done = bf16[256,7168]{1,0:T(8,128)(2,1)} async-done(((bf16[256,896]{1,0:T(8,128)(2,1)}), bf16[256,7168]{1,0:T(8,128)(2,1)}) %all-gather.2.cloned.1.call-update) | async-done | bytes 3670032 | tf_op jit(solution)/shard_map/all_gather | solution.py:102
  265.1 3.4 %multiply_reduce_fusion.2 = (f32[896]{0:T(1024)S(1)}, f32[896]{0:T(1024)S(1)}, f32[2048,896]{1,0:T(8,128)S(1)}) fusion(bf16[256,896]{0,1:T(8,128)(2,1)S(1)} %bitcast.29, bf16[256,7168]{1,0:T(8,128)(2,1)} %all-gather.2.cloned.1.call-done), kind=kOutput, calls=%fused_computation.6 | convolution fusion | flops 948697344 | bytes 8854528 | tf_op jit(solution)/shard_map/dot_general | solution.py:109
  268.5 2.2 multiply_reduce_fusion.1
  270.7 2.2 multiply_reduce_fusion
  272.9 1.1 multiply_reduce_fusion.4
  274.0 1.2 fusion.10
  275.2 1.2 fusion.33
  276.4 1.2 fusion.30
  277.5 0.0 copy-start.1
  277.6 0.8 fusion.39
  278.3 14.3 %all_to_all.22 = bf16[16,56,256]{2,1,0:T(8,128)(2,1)S(1)} all-to-all(bf16[16,56,256]{2,1,0:T(8,128)(2,1)S(1)} %bitcast.33), channel_id=1, replica_groups=mesh['client'=16,'unit'=8] {'client'}, dimensions={0} | all-to-all | bytes 917504 | tf_op jit(solution)/shard_map/all_to_all | solution.py:50
  292.7 0.1 reduce_sum.148
  292.7 0.8 broadcast_in_dim.5
  293.5 4.7 %all-to-all-start.3 = ((bf16[16,56,256]{2,1,0:T(8,128)(2,1)}), bf16[16,56,256]{2,1,0:T(8,128)(2,1)S(1)}, u32[]{:S(2)}, u32[]{:S(2)}) async-start(bf16[16,56,256]{2,1,0:T(8,128)(2,1)} %broadcast_in_dim.5), calls=%async_computation.3 | async-start | bytes 917504 | tf_op jit(solution)/shard_map/all_to_all | solution.py:36
  298.3 0.6 div.89
  298.9 8.4 %all-to-all-done.3 = bf16[16,56,256]{2,1,0:T(8,128)(2,1)S(1)} async-done(((bf16[16,56,256]{2,1,0:T(8,128)(2,1)}), bf16[16,56,256]{2,1,0:T(8,128)(2,1)S(1)}, u32[]{:S(2)}, u32[]{:S(2)}) %all-to-all-start.3) | async-done | bytes 458784 | tf_op jit(solution)/shard_map/all_to_all | solution.py:36
  307.2 1.0 convert_multiply_fusion
  (15 shorter events, 0.1 us)
Async XLA Ops:
  7.2 176.6 %copy-start = (bf16[256,896]{1,0:T(8,128)(2,1)S(1)}, bf16[256,896]{1,0:T(8,128)(2,1)}, u32[]{:S(2)}) copy-start(bf16[256,896]{1,0:T(8,128)(2,1)} %param.13) | copy-start | bytes 1376260
  7.2 163.3 %all-reduce.2.cloned.1.call-start = ((), (), s32[]{:S(2)}) async-start(), calls=%async_computation.4 | async-start | bytes 8388608 | tf_op jit(solution)/shard_map/psum | solution.py:85
  12.8 160.5 %copy-start.5 = (f32[4096]{0:T(1024)S(1)}, f32[4096]{0:T(1024)}, u32[]{:S(2)}) copy-start(f32[4096]{0:T(1024)} %param.9) | copy-start | bytes 49156
  12.8 252.3 %all-gather.2.cloned.1.call-start = ((), (), s32[]{:S(2)}) async-start(), calls=%async_computation.5 | async-start | bytes 4128768 | tf_op jit(solution)/shard_map/all_gather | solution.py:102
  170.5 3.4 %copy-start.2 = (f32[256,4096]{1,0:T(8,128)S(1)}, f32[256,4096]{1,0:T(8,128)}, u32[]{:S(2)}) copy-start(f32[256,4096]{1,0:T(8,128)} %all-reduce.2.cloned.1.call-done) | copy-start | bytes 12582916
  174.0 6.3 %slice-start = ((s8[7340032]{0:T(1024)(128)(4,1)}), s8[3145728]{0:T(1024)(128)(4,1)S(1)}, s32[]{:S(2)}) async-start(s8[7340032]{0:T(1024)(128)(4,1)} %bitcast.34), calls=%async_computation.6 | async-start | bytes 6291456
  174.5 5.7 %slice-start.1 = ((s8[7340032]{0:T(1024)(128)(4,1)}), s8[4194304]{0:T(1024)(128)(4,1)S(1)}, s32[]{:S(2)}) async-start(s8[7340032]{0:T(1024)(128)(4,1)} %bitcast.34), calls=%async_computation.7 | async-start | bytes 8388608
  182.8 1.4 copy-start.4
  265.1 3.4 %copy-start.3 = (bf16[256,7168]{1,0:T(8,128)(2,1)S(1)}, bf16[256,7168]{1,0:T(8,128)(2,1)}, u32[]{:S(2)}) copy-start(bf16[256,7168]{1,0:T(8,128)(2,1)} %all-gather.2.cloned.1.call-done) | copy-start | bytes 11010052
  277.5 30.6 %copy-start.1 = (bf16[256,896]{1,0:T(8,128)(2,1)S(1)}, bf16[256,896]{1,0:T(8,128)(2,1)}, u32[]{:S(2)}) copy-start(bf16[256,896]{1,0:T(8,128)(2,1)} %param.13) | copy-start | bytes 1376260
  293.5 13.7 %all-to-all-start.3 = ((bf16[16,56,256]{2,1,0:T(8,128)(2,1)}), bf16[16,56,256]{2,1,0:T(8,128)(2,1)S(1)}, u32[]{:S(2)}, u32[]{:S(2)}) async-start(bf16[16,56,256]{2,1,0:T(8,128)(2,1)} %broadcast_in_dim.5), calls=%async_computation.3 | async-start | bytes 917504 | tf_op jit(solution)/shard_map/all_to_all | solution.py:36
Sparse Core Ops, SparseCore 0:
  12.9 157.5 all-reduce.1
  183.9 81.1 all-gather.1
where the time goes:
time: 315 us
  waiting for transfers between devices  199 us (63%)
  blocking collectives  59.6 us (19%)
  matrix products  27.4 us (9%)
  between operations  14.3 us (5%)
  other arithmetic  6.02 us (2%)
  starting transfers between devices  4.82 us (2%)
  local copies, waits for them, and re-layouts  3.95 us (1%)
    psum x1, waiting for transfers between devices, body(): embedded = lax.psum(partial_rows, ('client', 'unit'))  158 us
    all_gather x1, waiting for transfers between devices, body(): segment = lax.all_gather(client_std, 'unit', axis=1, tiled=True)  32.9 us
    all_to_all x1, blocking collectives, summed_on_arrival(): blocks = lax.all_to_all(split_up(shard, dim, count), axis, 0, 0, tiled=True)  31.7 us
    all_to_all x1, blocking collectives, sent_and_summed(): lax.all_to_all(blocks, axis, split_axis=0, concat_axis=0, tiled=True)  14.3 us
    all_to_all x1, blocking collectives, copy_for_each(): return lax.all_to_all(copies, axis, split_axis=0, concat_axis=0, tiled=True)  13.6 us
    dot_general x4, matrix products, body(): jnp.dot(columns.T, ref_std, preferred_element_type=jnp.float32)  8.84 us
    all_to_all x1, waiting for transfers between devices, copy_for_each(): return lax.all_to_all(copies, axis, split_axis=0, concat_axis=0, tiled=True)  8.36 us
  transfers between devices with their start and end apart: 3, of which 3 were waited for; matrix products, arithmetic and copies ran while one was open for 1% of the time, Pallas kernels for 0%

commit v1 on v0

--- a/solution.py
+++ b/solution.py
@@ -82,7 +82,9 @@
     table_rows = table_start + jnp.arange(rows_here, dtype=jnp.int32)
     selector = (token_ids[:, None] == table_rows[None, :]).astype(jnp.bfloat16)
     partial_rows = jnp.dot(selector, embed_table, preferred_element_type=jnp.float32)
-    embedded = lax.psum(partial_rows, ("client", "unit"))
+    embedded = partial_rows
+    for rr in ("client", "unit"):
+        embedded = lax.psum(embedded, rr)
     normed = rms_scaled(embedded, norm_gain)
     token_count = normed.shape[0]
     inverse_tokens = 1.0 / token_count

time: 315 us -> 479 us (1.52)
  waiting for transfers between devices: 199 us -> 362 us
    psum x1 -> x2, waiting for transfers between devices: 158 us -> 321 us  [body(): embedded = lax.psum(embedded, rr)]
  transfers between devices with their start and end apart: 3 -> 4, of which waited for: 3 -> 4; matrix products, arithmetic and copies ran while one was open for 1% -> 1% of each run, Pallas kernels for 0% -> 0%
where the time goes in v1:
time: 479 us; the launch traced here: 478 us
  waiting for transfers between devices  362 us (76%)
  blocking collectives  60.1 us (13%)
  matrix products  27.4 us (6%)
  between operations  14 us (3%)
  other arithmetic  6.02 us (1%)
  starting transfers between devices  4.86 us (1%)
    psum x2, waiting for transfers between devices, body(): embedded = lax.psum(embedded, rr)  321 us
    all_gather x1, waiting for transfers between devices, body(): segment = lax.all_gather(client_std, 'unit', axis=1, tiled=True)  32.9 us
    all_to_all x1, blocking collectives, summed_on_arrival(): blocks = lax.all_to_all(split_up(shard, dim, count), axis, 0, 0, tiled=True)  32.1 us
    all_to_all x1, blocking collectives, sent_and_summed(): lax.all_to_all(blocks, axis, split_axis=0, concat_axis=0, tiled=True)  14.3 us
    all_to_all x1, blocking collectives, copy_for_each(): return lax.all_to_all(copies, axis, split_axis=0, concat_axis=0, tiled=True)  13.7 us
  transfers between devices with their start and end apart: 4, of which 4 were waited for; matrix products, arithmetic and copies ran while one was open for 1% of the time, Pallas kernels for 0%

profile of v1, /device:TPU:1, one launch (start us, length us, event | category | flops | bytes accessed | tf_op | source)
XLA Modules:
  0.0 478.4 jit_solution(14996742242532336033)
XLA Ops:
  7.2 0.0 copy-start
  7.2 0.0 all-reduce.3.cloned.1.call-start
  7.2 5.5 %fusion.51 = f32[256,4096]{1,0:T(8,128)} fusion(bf16[512,4096]{1,0:T(8,128)(2,1)} %param.8, s32[512]{0:T(512)S(1)} %iota_add_fusion, s32[256]{0:T(256)} %param.7), kind=kOutput, calls=%fused_computation.49 | convolution fusion | flops 1073872896 | bytes 8391680 | tf_op jit(solution)/shard_map/dot_general | solution.py:84
  12.8 0.0 all-reduce.3.cloned.1.call-update
  12.8 0.0 all-reduce.5.cloned.1.call-start
  12.8 132.0 %all-reduce.3.cloned.1.call-done = f32[256,4096]{1,0:T(8,128)} async-done(((f32[256,4096]{1,0:T(8,128)}), f32[256,4096]{1,0:T(8,128)}) %all-reduce.3.cloned.1.call-update) | async-done | bytes 4194320 | tf_op jit(solution)/shard_map/psum | solution.py:87
  144.9 0.0 all-reduce.5.cloned.1.call-update
  144.9 0.0 all-gather.2.cloned.1.call-start
  145.0 188.7 %all-reduce.5.cloned.1.call-done = f32[256,4096]{1,0:T(8,128)} async-done(((f32[256,4096]{1,0:T(8,128)}), f32[256,4096]{1,0:T(8,128)}) %all-reduce.5.cloned.1.call-update) | async-done | bytes 4194320 | tf_op jit(solution)/shard_map/psum | solution.py:87
  333.6 2.7 multiply_reduce_fusion.3
  336.3 0.0 copy-done.5
  336.3 0.7 copy-done.2
  337.1 0.6 multiply_convert_fusion
  337.7 0.0 slice-start.1
  337.7 5.7 %fusion.2 = f32[256,896]{1,0:T(8,128)S(1)} fusion(bf16[256,4096]{1,0:T(8,128)(2,1)S(1)} %multiply_convert_fusion, bf16[1,4096,896]{2,1,0:T(8,128)(2,1)} %param.10), kind=kOutput, calls=%fused_computation.2 | convolution fusion | flops 1879048192 | bytes 10354688 | tf_op jit(solution)/shard_map/dot_general | solution.py:91
  343.4 0.0 slice-done
  343.4 2.4 fusion.69
  345.9 0.0 copy-start.4
  345.9 0.1 multiply_reduce_fusion.5
  346.0 0.9 divide_convert_fusion
  346.9 0.0 all-gather.2.cloned.1.call-update
  346.9 0.3 fusion.58
  347.2 0.3 fusion.60
  347.5 0.1 pad_maximum_fusion
  347.7 1.8 copy.9
  349.4 32.1 %all_to_all.20 = f32[16,512,56]{1,2,0:T(8,128)S(1)} all-to-all(f32[16,512,56]{1,2,0:T(8,128)} %bitcast.27), channel_id=1, replica_groups=mesh['client'=16,'unit'=8] {'client'}, dimensions={0} | all-to-all | bytes 3670016 | tf_op jit(solution)/shard_map/all_to_all | solution.py:17
  381.6 0.1 reduce_sum.141
  381.7 0.1 fusion.68
  381.9 0.2 multiply_reduce_fusion.6
  382.1 0.1 divide_convert_fusion.1
  382.2 13.7 %all_to_all.21 = bf16[16,256,56]{1,2,0:T(8,128)(2,1)S(1)} all-to-all(bf16[16,256,56]{1,2,0:T(8,128)(2,1)S(1)} %broadcast_in_dim.4), channel_id=1, replica_groups=mesh['client'=16,'unit'=8] {'client'}, dimensions={0} | all-to-all | bytes 917504 | tf_op jit(solution)/shard_map/all_to_all | solution.py:36
  395.9 32.9 %all-gather.2.cloned.1.call-done = bf16[256,7168]{1,0:T(8,128)(2,1)} async-done(((bf16[256,896]{1,0:T(8,128)(2,1)}), bf16[256,7168]{1,0:T(8,128)(2,1)}) %all-gather.2.cloned.1.call-update) | async-done | bytes 3670032 | tf_op jit(solution)/shard_map/all_gather | solution.py:104
  428.8 3.4 multiply_reduce_fusion.2
  432.2 2.2 multiply_reduce_fusion.1
  434.4 2.2 multiply_reduce_fusion
  436.6 1.1 multiply_reduce_fusion.4
  437.7 1.2 fusion.10
  438.9 1.2 fusion.33
  440.1 1.2 fusion.30
  441.2 0.0 copy-start.1
  441.2 0.8 fusion.39
  442.0 14.3 %all_to_all.22 = bf16[16,56,256]{2,1,0:T(8,128)(2,1)S(1)} all-to-all(bf16[16,56,256]{2,1,0:T(8,128)(2,1)S(1)} %bitcast.33), channel_id=1, replica_groups=mesh['client'=16,'unit'=8] {'client'}, dimensions={0} | all-to-all | bytes 917504 | tf_op jit(solution)/shard_map/all_to_all | solution.py:50
  456.3 0.1 reduce_sum.148
  456.4 0.8 broadcast_in_dim.5
  457.2 4.7 all-to-all-start.3
  461.9 0.6 div.89
  462.5 8.4 %all-to-all-done.3 = bf16[16,56,256]{2,1,0:T(8,128)(2,1)S(1)} async-done(((bf16[16,56,256]{2,1,0:T(8,128)(2,1)}), bf16[16,56,256]{2,1,0:T(8,128)(2,1)S(1)}, u32[]{:S(2)}, u32[]{:S(2)}) %all-to-all-start.3) | async-done | bytes 458784 | tf_op jit(solution)/shard_map/all_to_all | solution.py:36
  470.9 1.0 convert_multiply_fusion
  (18 shorter events, 0.1 us)
Async XLA Ops:
  7.2 339.8 %copy-start = (bf16[256,896]{1,0:T(8,128)(2,1)S(1)}, bf16[256,896]{1,0:T(8,128)(2,1)}, u32[]{:S(2)}) copy-start(bf16[256,896]{1,0:T(8,128)(2,1)} %param.13) | copy-start | bytes 1376260
  7.2 137.7 %all-reduce.3.cloned.1.call-start = ((), (), s32[]{:S(2)}) async-start(), calls=%async_computation.4 | async-start | bytes 8388608 | tf_op jit(solution)/shard_map/psum | solution.py:87
  12.8 320.8 %all-reduce.5.cloned.1.call-start = ((), (), s32[]{:S(2)}) async-start(), calls=%async_computation.5 | async-start | bytes 8388608 | tf_op jit(solution)/shard_map/psum | solution.py:87
  144.9 191.5 %copy-start.5 = (f32[4096]{0:T(1024)S(1)}, f32[4096]{0:T(1024)}, u32[]{:S(2)}) copy-start(f32[4096]{0:T(1024)} %param.9) | copy-start | bytes 49156
  144.9 283.9 %all-gather.2.cloned.1.call-start = ((), (), s32[]{:S(2)}) async-start(), calls=%async_computation.6 | async-start | bytes 4128768 | tf_op jit(solution)/shard_map/all_gather | solution.py:104
  333.6 3.4 copy-start.2
  337.1 6.3 %slice-start = ((s8[7340032]{0:T(1024)(128)(4,1)}), s8[3145728]{0:T(1024)(128)(4,1)S(1)}, s32[]{:S(2)}) async-start(s8[7340032]{0:T(1024)(128)(4,1)} %bitcast.34), calls=%async_computation.7 | async-start | bytes 6291456
  337.7 5.7 %slice-start.1 = ((s8[7340032]{0:T(1024)(128)(4,1)}), s8[4194304]{0:T(1024)(128)(4,1)S(1)}, s32[]{:S(2)}) async-start(s8[7340032]{0:T(1024)(128)(4,1)} %bitcast.34), calls=%async_computation.8 | async-start | bytes 8388608
  345.9 1.4 copy-start.4
  428.8 3.4 copy-start.3
  441.2 30.6 %copy-start.1 = (bf16[256,896]{1,0:T(8,128)(2,1)S(1)}, bf16[256,896]{1,0:T(8,128)(2,1)}, u32[]{:S(2)}) copy-start(bf16[256,896]{1,0:T(8,128)(2,1)} %param.13) | copy-start | bytes 1376260
  457.2 13.7 %all-to-all-start.3 = ((bf16[16,56,256]{2,1,0:T(8,128)(2,1)}), bf16[16,56,256]{2,1,0:T(8,128)(2,1)S(1)}, u32[]{:S(2)}, u32[]{:S(2)}) async-start(bf16[16,56,256]{2,1,0:T(8,128)(2,1)} %broadcast_in_dim.5), calls=%async_computation.3 | async-start | bytes 917504 | tf_op jit(solution)/shard_map/all_to_all | solution.py:36
Sparse Core Ops, SparseCore 0:
  12.9 131.9 all-reduce.2
  147.4 186.1 all-reduce.4
  347.0 81.7 all-gather.1
